TPU v7x, 32 devices: a whole 2x2x4 slice. The times are simulated.
32 devices in a mesh: ep: 8 (over y, x, core), dp: 4 (over z).
Axes of the slice: x: 2, y: 2, z: 4, core: 2. Of those that a mesh axis runs over, the one named last changes fastest.
Arguments:
- out_grad: bfloat16 [4, 1024, 2048], P('dp', 'ep'), may hold values from -6 to 6
- gates: bfloat16 [4, 1024, 8], P('dp', 'ep'), may hold values from 0.019897461 to 0.5
- routes: int32 [4, 1024, 8], P('dp', 'ep'), may hold values from 0 to 31, all different within a row; in each aligned block of 128 rows (0 to 127, 128 to 255, ..., all dimensions but the last counted through in order) at most 48 rows name the same one
- expert_slot: int32 [32], replicated, may hold values from 0 to 31, each once
- hidden_saved: bfloat16 [4, 32, 8, 48, 768], P('dp', 'ep'), may hold values from -6 to 6
- w_down: bfloat16 [2048, 24576], P('dp', 'ep'), may hold values from -0.21875 to 0.21875
Outputs:
- hidden_grad: bfloat16 [4, 32, 8, 48, 768], P('dp', 'ep')
- gate_grad: float32 [4, 1024, 8], P('dp', 'ep')
- weight_grad: float32 [2048, 24576], P('dp', 'ep')
Inputs may be any that keep to these rules, and one draw needn't show every extreme that they name: `routes`: the rows of one device name no expert more than 48 times, and every expert is named by some row. `expert_slot`: each slot once.
All inputs are finite; a program needn't handle non-finite values.
Results may differ from a plain program's by a relative error of at most 0.012.
Values may be sent and summed in bfloat16 or wider, within the bound.
No kernel may reach another device: no remote copies, remote signals or barrier semaphores. Data moves between devices by JAX's collectives and lax.ppermute only.
A program may use at most 128 MiB of HBM per device.

v0:
```python
import jax
import jax.numpy as jnp
from jax import lax
from jax.sharding import PartitionSpec as P


def local(out_grad, gates, routes, expert_slot, hidden_saved, w_down):
    tokens = out_grad.shape[1]
    width = out_grad.shape[2]
    chosen = routes.shape[2]
    experts = expert_slot.shape[0]
    n_ep = lax.axis_size("ep")
    exp_dev = experts // n_ep
    slots = hidden_saved.shape[3]
    hidden = hidden_saved.shape[4]
    flat_ids = routes.reshape(-1)
    onehot = (flat_ids[:, None] == jnp.arange(experts, dtype=jnp.int32)[None, :]).astype(jnp.int32)
    slot_ids = jnp.sum(onehot * expert_slot[None, :], axis=1)
    ranks = jnp.sum(onehot * (jnp.cumsum(onehot, axis=0) - 1), axis=1)
    target = slot_ids * slots + ranks
    rows = jnp.repeat(out_grad[0], chosen, axis=0)
    send_rows = jnp.zeros((experts * slots, width), jnp.bfloat16).at[target].set(rows)
    send_gates = jnp.zeros((experts * slots,), jnp.bfloat16).at[target].set(gates.reshape(-1))
    recv_rows, recv_gates = (
        lax.all_to_all(
            send_rows.reshape(n_ep, exp_dev * slots, width),
            "ep",
            split_axis=0,
            concat_axis=0,
            tiled=True,
        ),
        lax.all_to_all(
            send_gates.reshape(n_ep, exp_dev * slots), "ep", split_axis=0, concat_axis=0, tiled=True
        ),
    )
    recv_rows = recv_rows.reshape(n_ep, exp_dev, slots, width)
    saved = hidden_saved[0]
    w_all = lax.all_gather(w_down, "dp", axis=0, tiled=True).reshape(width, exp_dev, hidden)
    upstream = jnp.einsum("slcd,dlj->lscj", recv_rows, w_all, preferred_element_type=jnp.float32)
    gates_lsc = recv_gates.reshape(n_ep, exp_dev, slots).transpose(1, 0, 2).astype(jnp.float32)
    hidden_grad = (gates_lsc[..., None] * upstream).astype(jnp.bfloat16)[None]
    slot_grad = jnp.sum(saved.astype(jnp.float32) * upstream, axis=3)
    returned = lax.all_to_all(
        slot_grad.transpose(1, 0, 2).reshape(n_ep, exp_dev * slots),
        "ep",
        split_axis=0,
        concat_axis=0,
        tiled=True,
    )
    gate_grad = returned.reshape(-1)[target].reshape(1, tokens, chosen)
    scaled = (gates_lsc[..., None] * saved.astype(jnp.float32)).astype(jnp.bfloat16)
    term = jnp.einsum("slcd,lscj->dlj", recv_rows, scaled, preferred_element_type=jnp.float32)
    weight_grad = lax.psum_scatter(
        term.reshape(width // lax.axis_size("dp") * lax.axis_size("dp"), exp_dev * hidden).astype(
            jnp.bfloat16
        ),
        "dp",
        scatter_dimension=0,
        tiled=True,
    ).astype(jnp.float32)
    return (hidden_grad, gate_grad, weight_grad)


def solution(mesh):
    return jax.shard_map(
        local,
        mesh=mesh,
        in_specs=(
            P("dp", "ep", None),
            P("dp", "ep", None),
            P("dp", "ep", None),
            P(),
            P("dp", "ep", None, None, None),
            P("dp", "ep"),
        ),
        out_specs=(P("dp", "ep", None, None, None), P("dp", "ep", None), P("dp", "ep")),
        check_vma=False,
    )
```

profile of v0, /device:TPU:0, one launch (start us, length us, event | category | flops | bytes accessed | tf_op | source)
XLA Modules:
  0.0 457.8 jit_solution(12318421995495534040)
XLA Ops:
  7.2 0.0 copy-start
  7.2 0.0 copy-start.2
  7.2 0.0 copy-start.3
  7.2 0.0 copy-start.4
  7.2 0.0 all-gather.2.cloned.1.call-start
  7.3 4.7 %copy.29 = bf16[512,3072]{0,1:T(8,128)(2,1)} copy(bf16[512,3072]{1,0:T(8,128)(2,1)} %param.11) | data formatting | bytes 6291456 | tf_op args[5]
  12.0 0.0 all-gather.2.cloned.1.call-update
  12.0 0.0 copy-done.2
  12.0 0.1 copy.22
  12.1 0.1 eq.29
  12.2 0.1 eq.25
  12.3 0.0 copy-done.3
  12.3 0.1 copy.26
  12.4 0.1 reshape.113
  12.5 9.0 %reduce-window.6 = s32[32,8,128]{2,1,0:T(8,128)S(1)} reduce-window(s32[32,8,128]{2,1,0:T(8,128)S(1)} %fusion.15, s32[]{:T(128)} %constant.7.clone.1), window={size=1x1x128 pad=0_0x0_0x127_0}, to_apply=%region_1.0 | reduce-window | flops 4161536 | bytes 262148 | tf_op jit(solution)/shard_map/reduce-window
  21.6 0.1 slice.10
  21.7 0.1 copy.24
  21.8 0.1 copy.25
  21.9 0.1 add_add_fusion
  22.0 0.0 copy-done.4
  22.0 0.1 select_reduce_fusion
  22.1 7.6 %scatter_custom_fusion = bf16[1536]{0:T(1024)(128)(2,1)S(1)} fusion(s32[1024]{0:T(1024)S(1)} %bitcast.55, bf16[1024]{0:T(1024)(128)(2,1)S(1)} %reshape.113, bf16[]{:T(256)} %constant.6.clone.1), kind=kCustom, calls=%fused_computation.31 | custom fusion | bytes 3074 | tf_op jit(solution)/shard_map/scatter | solution.py:23
  29.7 0.7 all_to_all.20
  30.4 5.2 %all-to-all-start = ((bf16[8,1,192]{2,1,0:T(2,128)(2,1)}), bf16[8,1,192]{2,1,0:T(2,128)(2,1)S(1)}, u32[]{:S(2)}, u32[]{:S(2)}) async-start(bf16[8,1,192]{2,1,0:T(2,128)(2,1)} %all_to_all.20), calls=%async_computation | async-start | bytes 16384 | tf_op jit(solution)/shard_map/all_to_all | solution.py:32
  35.6 0.0 copy-done
  35.6 10.2 %scatter_custom_fusion.1 = bf16[1536,2048]{1,0:T(8,128)(2,1)} fusion(s32[1024]{0:T(1024)S(1)} %bitcast.56, bf16[]{:T(256)} %constant.6.clone.1, bf16[128,2048]{1,0:T(8,128)(2,1)S(1)} %bitcast.47), kind=kCustom, calls=%fused_computation.12 | custom fusion | bytes 6815746 | tf_op jit(solution)/shard_map/scatter | solution.py:22
  45.9 0.0 all-to-all-done
  45.9 4.9 %all-to-all-start.1 = ((bf16[8,192,2048]{2,1,0:T(8,128)(2,1)}), bf16[8,192,2048]{2,1,0:T(8,128)(2,1)}, u32[]{:S(2)}, u32[]{:S(2)}) async-start(bf16[8,192,2048]{2,1,0:T(8,128)(2,1)} %bitcast.48), calls=%async_computation.1 | async-start | bytes 12582912 | tf_op jit(solution)/shard_map/all_to_all | solution.py:25
  50.8 0.2 reduce-scatter.2.cloned.1.call-start
  51.1 0.1 reshape.100
  51.1 71.2 %all-to-all-done.1 = bf16[8,192,2048]{2,1,0:T(8,128)(2,1)} async-done(((bf16[8,192,2048]{2,1,0:T(8,128)(2,1)}), bf16[8,192,2048]{2,1,0:T(8,128)(2,1)}, u32[]{:S(2)}, u32[]{:S(2)}) %all-to-all-start.1) | async-done | bytes 6291488 | tf_op jit(solution)/shard_map/all_to_all | solution.py:25
  122.4 0.0 copy-done.5
  122.4 12.5 %bitcast_convert_fusion = bf16[4,768,2048]{2,1,0:T(8,128)(2,1)} fusion(bf16[8,4,48,2048]{3,2,1,0:T(8,128)(2,1)} %bitcast.8, bf16[1,4,8,48,768]{4,3,2,1,0:T(8,128)(2,1)S(1)} %copy-done.5, f32[4,8,48]{2,1,0:T(8,128)S(1)} %copy.28), kind=kOutput, calls=%fused_computation.3 | convolution fusion | flops 4841668608 | bytes 21239808 | tf_op jit(solution)/shard_map/slcd,lscj->dlj/dot_general | solution.py:52
  134.9 16.7 %copy.35 = bf16[2048,3072]{1,0:T(8,128)(2,1)} copy(bf16[2048,3072]{0,1:T(8,128)(2,1)} %bitcast.49) | data formatting | bytes 25165824 | tf_op jit(solution)/shard_map/convert_element_type | solution.py:54
  151.6 0.0 reduce-scatter.2.cloned.1.call-update
  151.6 81.4 %all-gather.2.cloned.1.call-done = bf16[2048,3072]{0,1:T(8,128)(2,1)} async-done(((bf16[512,3072]{0,1:T(8,128)(2,1)}), bf16[2048,3072]{0,1:T(8,128)(2,1)}) %all-gather.2.cloned.1.call-update) | async-done | bytes 12582928 | tf_op jit(solution)/shard_map/all_gather | solution.py:38
  233.1 15.4 %fusion.3 = (f32[4,8,48]{2,1,0:T(8,128)S(1)}, bf16[1,4,8,48,768]{4,3,2,1,0:T(8,128)(2,1)}) fusion(bf16[1,4,8,48,768]{4,3,2,1,0:T(8,128)(2,1)S(1)} %copy-done.5, f32[4,8,48]{2,1,0:T(8,128)S(1)} %copy.28, bf16[2048,4,768,1]{0,2,3,1:T(8,128)(2,1)} %bitcast.58, bf16[8,4,48,2048]{3,2,1,0:T(8,128)(2,1)} %bitcast.8), kind=kOutput, calls=%fused_computation.9 | convolution fusion | flops 4837734912 | bytes 23605248 | tf_op jit(solution)/shard_map/slcd,dlj->lscj/dot_general | solution.py:39
  248.5 0.7 all_to_all.21
  249.2 3.7 all-to-all-start.2
  252.9 4.7 %all-to-all-done.2 = f32[8,1,192]{2,1,0:T(1,128)S(1)} async-done(((f32[8,1,192]{2,1,0:T(1,128)}), f32[8,1,192]{2,1,0:T(1,128)S(1)}, u32[]{:S(2)}, u32[]{:S(2)}) %all-to-all-start.2) | async-done | bytes 6176 | tf_op jit(solution)/shard_map/all_to_all | solution.py:43
  257.6 0.0 copy-start.1
  257.6 0.1 reshape.97
  257.7 6.1 %gather_fusion = f32[1024]{0:T(1024)S(1)} fusion(f32[1536]{0:T(1024)S(1)} %reshape.97, s32[1024]{0:T(1024)S(1)} %broadcast_clamp_fusion), kind=kCustom, calls=%fused_computation | custom fusion | bytes 12288 | tf_op jit(solution)/shard_map/gather | solution.py:50
  263.8 0.1 reshape.98
  263.9 0.7 copy.36
  264.6 180.9 %reduce-scatter.2.cloned.1.call-done = bf16[512,3072]{1,0:T(8,128)(2,1)} async-done(((bf16[2048,3072]{1,0:T(8,128)(2,1)}), bf16[512,3072]{1,0:T(8,128)(2,1)}) %reduce-scatter.2.cloned.1.call-update) | async-done | bytes 3145744 | tf_op jit(solution)/shard_map/reduce_scatter | solution.py:53
  445.5 5.4 %convert_element_type.50 = f32[512,3072]{1,0:T(8,128)} convert(bf16[512,3072]{1,0:T(8,128)(2,1)} %reduce-scatter.2.cloned.1.call-done) | non-fusion elementwise | flops 1572864 | bytes 9437184 | tf_op jit(solution)/shard_map/convert_element_type | solution.py:60
  450.9 0.0 copy-done.1
  (11 shorter events, 0.1 us)
Async XLA Ops:
  7.2 28.5 %copy-start = (bf16[1,128,2048]{2,1,0:T(8,128)(2,1)S(1)}, bf16[1,128,2048]{2,1,0:T(8,128)(2,1)}, u32[]{:S(2)}) copy-start(bf16[1,128,2048]{2,1,0:T(8,128)(2,1)} %param.6) | copy-start | bytes 1572868
  7.2 4.8 %copy-start.2 = (s32[1,128,8]{1,2,0:T(8,128)S(1)}, s32[1,128,8]{1,2,0:T(8,128)}, u32[]{:S(2)}) copy-start(s32[1,128,8]{1,2,0:T(8,128)} %param.8) | copy-start | bytes 12292
  7.2 5.1 %copy-start.3 = (bf16[1,128,8]{1,2,0:T(8,128)(2,1)S(1)}, bf16[1,128,8]{1,2,0:T(8,128)(2,1)}, u32[]{:S(2)}) copy-start(bf16[1,128,8]{1,2,0:T(8,128)(2,1)} %param.7) | copy-start | bytes 6148
  7.2 14.8 %copy-start.4 = (s32[32]{0:T(128)S(1)}, s32[32]{0:T(128)}, u32[]{:S(2)}) copy-start(s32[32]{0:T(128)} %param.9) | copy-start | bytes 388
  7.2 225.8 %all-gather.2.cloned.1.call-start = ((), (), s32[]{:S(2)}) async-start(), calls=%async_computation.4 | async-start | bytes 15728640 | tf_op jit(solution)/shard_map/all_gather | solution.py:38
  30.4 15.5 %all-to-all-start = ((bf16[8,1,192]{2,1,0:T(2,128)(2,1)}), bf16[8,1,192]{2,1,0:T(2,128)(2,1)S(1)}, u32[]{:S(2)}, u32[]{:S(2)}) async-start(bf16[8,1,192]{2,1,0:T(2,128)(2,1)} %all_to_all.20), calls=%async_computation | async-start | bytes 16384 | tf_op jit(solution)/shard_map/all_to_all | solution.py:32
  45.9 76.5 %copy-start.5 = (bf16[1,4,8,48,768]{4,3,2,1,0:T(8,128)(2,1)S(1)}, bf16[1,4,8,48,768]{4,3,2,1,0:T(8,128)(2,1)}, u32[]{:S(2)}) copy-start(bf16[1,4,8,48,768]{4,3,2,1,0:T(8,128)(2,1)} %param.10) | copy-start | bytes 7077892
  45.9 76.5 %all-to-all-start.1 = ((bf16[8,192,2048]{2,1,0:T(8,128)(2,1)}), bf16[8,192,2048]{2,1,0:T(8,128)(2,1)}, u32[]{:S(2)}, u32[]{:S(2)}) async-start(bf16[8,192,2048]{2,1,0:T(8,128)(2,1)} %bitcast.48), calls=%async_computation.1 | async-start | bytes 12582912 | tf_op jit(solution)/shard_map/all_to_all | solution.py:25
  50.8 394.7 %reduce-scatter.2.cloned.1.call-start = ((), (), s32[]{:S(2)}) async-start(), calls=%async_computation.5 | async-start | bytes 15728640 | tf_op jit(solution)/shard_map/reduce_scatter | solution.py:53
  249.2 8.4 %all-to-all-start.2 = ((f32[8,1,192]{2,1,0:T(1,128)}), f32[8,1,192]{2,1,0:T(1,128)S(1)}, u32[]{:S(2)}, u32[]{:S(2)}) async-start(f32[8,1,192]{2,1,0:T(1,128)} %all_to_all.21), calls=%async_computation.2 | async-start | bytes 16384 | tf_op jit(solution)/shard_map/all_to_all | solution.py:43
  257.6 193.3 %copy-start.1 = (bf16[1,128,2048]{2,1,0:T(8,128)(2,1)S(1)}, bf16[1,128,2048]{2,1,0:T(8,128)(2,1)}, u32[]{:S(2)}) copy-start(bf16[1,128,2048]{2,1,0:T(8,128)(2,1)} %param.6) | copy-start | bytes 1572868
Sparse Core Ops, SparseCore 0:
  12.1 220.9 all-gather.1
  235.4 210.0 reduce-scatter.1
where the time goes:
time: 459 us; the launch traced here: 458 us
  waiting for transfers between devices  338 us (74%)
  local copies, waits for them, and re-layouts  48.5 us (11%)
  matrix products  28 us (6%)
  other arithmetic  14.7 us (3%)
  between operations  14.2 us (3%)
  starting transfers between devices  14 us (3%)
    reduce_scatter x1, waiting for transfers between devices, local(): lax.psum_scatter(term.reshape(width // lax.axis_size('dp') * lax.axis_siz...  181 us
    all_gather x1, waiting for transfers between devices, local(): lax.all_gather(w_down, 'dp', axis=0, tiled=True)  81.4 us
    all_to_all x1, waiting for transfers between devices, local(): lax.all_to_all(send_rows.reshape(n_ep, exp_dev * slots, width), 'ep', spl...  71.2 us
    convert_element_type x1, local copies, waits for them, and re-layouts, local(): term.reshape(width // lax.axis_size('dp') * lax.axis_size('dp'), exp_dev...  16.7 us
    dot_general x1, matrix products, local(): jnp.einsum('slcd,dlj->lscj', recv_rows, w_all, preferred_element_type=jnp...  15.4 us
    dot_general x1, matrix products, local(): jnp.einsum('slcd,lscj->dlj', recv_rows, scaled, preferred_element_type=jn...  12.5 us
    scatter x1, local copies, waits for them, and re-layouts, local(): jnp.zeros((experts * slots, width), jnp.bfloat16).at[target].set(rows)  10.2 us
  transfers between devices with their start and end apart: 5, of which 4 were waited for; matrix products, arithmetic and copies ran while one was open for 17% of the time, Pallas kernels for 0%

commit v1 on v0

--- a/solution.py
+++ b/solution.py
@@ -2,6 +2,17 @@
 import jax.numpy as jnp
 from jax import lax
 from jax.sharding import PartitionSpec as P
+
+
+def ring_gather(shard, axis, dim):
+    ways = lax.axis_size(axis)
+    pieces = [shard]
+    for far in range(1, ways):
+        pieces.append(
+            lax.ppermute(pieces[far - 1], axis, [(d, (d - 1) % ways) for d in range(ways)])
+        )
+    line = jnp.concatenate(pieces, axis=dim)
+    return jnp.roll(line, lax.axis_index(axis) * shard.shape[dim], axis=dim)
 
 
 def local(out_grad, gates, routes, expert_slot, hidden_saved, w_down):
@@ -35,7 +46,7 @@
     )
     recv_rows = recv_rows.reshape(n_ep, exp_dev, slots, width)
     saved = hidden_saved[0]
-    w_all = lax.all_gather(w_down, "dp", axis=0, tiled=True).reshape(width, exp_dev, hidden)
+    w_all = ring_gather(w_down, "dp", 0).reshape(width, exp_dev, hidden)
     upstream = jnp.einsum("slcd,dlj->lscj", recv_rows, w_all, preferred_element_type=jnp.float32)
     gates_lsc = recv_gates.reshape(n_ep, exp_dev, slots).transpose(1, 0, 2).astype(jnp.float32)
     hidden_grad = (gates_lsc[..., None] * upstream).astype(jnp.bfloat16)[None]

time: 459 us -> 618 us (1.35)
  waiting for transfers between devices: 338 us -> 471 us
  local copies, waits for them, and re-layouts: 48.5 us -> 68.3 us
    ppermute x0 -> x3, waiting for transfers between devices: none -> 395 us  [ring_gather(): lax.ppermute(pieces[far - 1], axis, [(d, (d - 1) % ways) for d in range(w...]
    reduce_scatter x1, waiting for transfers between devices: 181 us -> 0.01 us  [local(): lax.psum_scatter(term.reshape(width // lax.axis_size('dp') * lax.axis_siz...]
    all_gather x1 -> x0, waiting for transfers between devices: 81.4 us -> none  [local(): lax.all_gather(w_down, 'dp', axis=0, tiled=True)]
    unnamed x16 -> x23, local copies, waits for them, and re-layouts: 5.62 us -> 17.7 us
  transfers between devices with their start and end apart: 5 -> 7, of which waited for: 4 -> 5; matrix products, arithmetic and copies ran while one was open for 17% -> 9% of each run, Pallas kernels for 0% -> 0%
where the time goes in v1:
time: 618 us; the launch traced here: 617 us
  waiting for transfers between devices  471 us (76%)
  local copies, waits for them, and re-layouts  68.3 us (11%)
  matrix products  28 us (5%)
  starting transfers between devices  19.9 us (3%)
  other arithmetic  15.4 us (2%)
  between operations  14.2 us (2%)
    ppermute x3, waiting for transfers between devices, ring_gather(): lax.ppermute(pieces[far - 1], axis, [(d, (d - 1) % ways) for d in range(w...  395 us
    all_to_all x1, waiting for transfers between devices, local(): lax.all_to_all(send_rows.reshape(n_ep, exp_dev * slots, width), 'ep', spl...  71.2 us
    unnamed x23, local copies, waits for them, and re-layouts  17.7 us
    convert_element_type x1, local copies, waits for them, and re-layouts, local(): term.reshape(width // lax.axis_size('dp') * lax.axis_size('dp'), exp_dev...  16.6 us
    dot_general x1, matrix products, local(): jnp.einsum('slcd,dlj->lscj', recv_rows, w_all, preferred_element_type=jnp...  15.4 us
    dot_general x1, matrix products, local(): jnp.einsum('slcd,lscj->dlj', recv_rows, scaled, preferred_element_type=jn...  12.6 us
  transfers between devices with their start and end apart: 7, of which 5 were waited for; matrix products, arithmetic and copies ran while one was open for 9% of the time, Pallas kernels for 0%

profile of v1, /device:TPU:0, one launch (start us, length us, event | category | flops | bytes accessed | tf_op | source)
XLA Modules:
  0.0 617.1 jit_solution(15990041486953764213)
XLA Ops:
  7.2 0.0 copy-start
  7.2 0.8 copy.24
  8.0 0.1 eq.32
  8.1 0.1 eq.28
  8.2 9.0 %reduce-window.6 = s32[32,8,128]{2,1,0:T(8,128)S(1)} reduce-window(s32[32,8,128]{2,1,0:T(8,128)S(1)} %fusion.15, s32[]{:T(128)} %constant.37.clone.1), window={size=1x1x128 pad=0_0x0_0x127_0}, to_apply=%region_1.0 | reduce-window | flops 4161536 | bytes 262148 | tf_op jit(solution)/shard_map/reduce-window
  17.2 0.1 slice.10
  17.3 0.1 copy.26
  17.5 0.1 copy.27
  17.6 0.1 add_add_fusion
  17.7 0.7 select_reduce_fusion
  18.5 0.8 copy.28
  19.3 0.1 reshape.113
  19.4 7.6 %scatter_custom_fusion = bf16[1536]{0:T(1024)(128)(2,1)S(1)} fusion(s32[1024]{0:T(1024)S(1)} %bitcast.54, bf16[1024]{0:T(1024)(128)(2,1)S(1)} %reshape.113, bf16[]{:T(256)} %constant.36.clone.1), kind=kCustom, calls=%fused_computation.39 | custom fusion | bytes 3074 | tf_op jit(solution)/shard_map/scatter | solution.py:34
  27.0 0.7 all_to_all.20
  27.7 5.2 all-to-all-start
  32.9 10.2 %scatter_custom_fusion.1 = bf16[1536,2048]{1,0:T(8,128)(2,1)} fusion(s32[1024]{0:T(1024)S(1)} %bitcast.55, bf16[]{:T(256)} %constant.36.clone.1, bf16[128,2048]{1,0:T(8,128)(2,1)S(1)} %bitcast.45), kind=kCustom, calls=%fused_computation.12 | custom fusion | bytes 6815746 | tf_op jit(solution)/shard_map/scatter | solution.py:33
  43.1 4.9 all-to-all-start.1
  48.1 0.2 reduce-scatter.2.cloned.1.call-start
  48.3 0.1 reshape.100
  48.4 71.2 %all-to-all-done.1 = bf16[8,192,2048]{2,1,0:T(8,128)(2,1)} async-done(((bf16[8,192,2048]{2,1,0:T(8,128)(2,1)}), bf16[8,192,2048]{2,1,0:T(8,128)(2,1)}, u32[]{:S(2)}, u32[]{:S(2)}) %all-to-all-start.1) | async-done | bytes 6291488 | tf_op jit(solution)/shard_map/all_to_all | solution.py:36
  119.6 12.6 %bitcast_convert_fusion = bf16[4,768,2048]{2,1,0:T(8,128)(2,1)} fusion(bf16[8,4,48,2048]{3,2,1,0:T(8,128)(2,1)} %bitcast.8, bf16[1,4,8,48,768]{4,3,2,1,0:T(8,128)(2,1)S(1)} %copy-done.4, f32[4,8,48]{2,1,0:T(8,128)S(1)} %copy.30), kind=kOutput, calls=%fused_computation.3 | convolution fusion | flops 4841668608 | bytes 21239808 | tf_op jit(solution)/shard_map/slcd,lscj->dlj/dot_general | solution.py:63
  132.2 16.6 %copy.39 = bf16[2048,3072]{1,0:T(8,128)(2,1)} copy(bf16[2048,3072]{0,1:T(8,128)(2,1)} %bitcast.47) | data formatting | bytes 25165824 | tf_op jit(solution)/shard_map/convert_element_type | solution.py:65
  148.8 0.0 reduce-scatter.2.cloned.1.call-update
  148.8 3.2 copy.32
  152.0 3.6 collective-permute-start
  155.7 191.2 %collective-permute-done = bf16[512,3072]{0,1:T(8,128)(2,1)S(1)} collective-permute-done((bf16[512,3072]{0,1:T(8,128)(2,1)S(1)}, bf16[512,3072]{0,1:T(8,128)(2,1)S(1)}, u32[]{:S(2)}, u32[]{:S(2)}) %collective-permute-start) | collective-permute-done | bytes 3145760 | tf_op jit(solution)/shard_map/ppermute | solution.py:12
  346.9 1.7 copy-done.2
  348.6 142.0 %collective-permute-done.1 = bf16[512,3072]{0,1:T(8,128)(2,1)} collective-permute-done((bf16[512,3072]{0,1:T(8,128)(2,1)S(1)}, bf16[512,3072]{0,1:T(8,128)(2,1)}, u32[]{:S(2)}, u32[]{:S(2)}) %collective-permute-start.1) | collective-permute-done | bytes 3145760 | tf_op jit(solution)/shard_map/ppermute | solution.py:12
  490.5 0.5 constant_dynamic-update-slice_fusion.7
  491.0 1.4 copy-done.3
  492.4 0.5 constant_dynamic-update-slice_fusion.6
  492.9 2.4 constant_dynamic-update-slice_fusion.5
  495.3 62.2 %collective-permute-done.2 = bf16[512,3072]{0,1:T(8,128)(2,1)} collective-permute-done((bf16[512,3072]{0,1:T(8,128)(2,1)}, bf16[512,3072]{0,1:T(8,128)(2,1)}, u32[]{:S(2)}, u32[]{:S(2)}) %collective-permute-start.2) | collective-permute-done | bytes 3145760 | tf_op jit(solution)/shard_map/ppermute | solution.py:12
  557.5 2.4 constant_dynamic-update-slice_fusion.4
  559.9 0.5 constant_dynamic-update-slice_fusion.3
  560.4 0.5 constant_dynamic-update-slice_fusion.2
  560.9 2.4 constant_dynamic-update-slice_fusion.1
  563.3 2.4 constant_dynamic-update-slice_fusion
  565.7 5.5 constant_dynamic-slice_fusion
  571.1 15.4 %fusion.3 = (f32[4,8,48]{2,1,0:T(8,128)S(1)}, bf16[1,4,8,48,768]{4,3,2,1,0:T(8,128)(2,1)}) fusion(bf16[1,4,8,48,768]{4,3,2,1,0:T(8,128)(2,1)S(1)} %copy-done.5, f32[4,8,48]{2,1,0:T(8,128)S(1)} %copy.30, bf16[2048,4,768,1]{0,2,3,1:T(8,128)(2,1)} %bitcast.48, bf16[8,4,48,2048]{3,2,1,0:T(8,128)(2,1)} %bitcast.8), kind=kOutput, calls=%fused_computation.9 | convolution fusion | flops 4837734912 | bytes 23605248 | tf_op jit(solution)/shard_map/slcd,dlj->lscj/dot_general | solution.py:50
  586.6 0.7 all_to_all.21
  587.2 5.9 all-to-all-start.2
  593.2 4.7 all-to-all-done.2
  597.9 0.1 reshape.97
  598.0 6.1 gather_fusion
  604.1 0.1 reshape.98
  604.2 0.7 copy.40
  604.9 5.4 convert_element_type.50
  (23 shorter events, 0.2 us)
Async XLA Ops:
  7.2 25.7 %copy-start = (bf16[1,128,2048]{2,1,0:T(8,128)(2,1)S(1)}, bf16[1,128,2048]{2,1,0:T(8,128)(2,1)}, u32[]{:S(2)}) copy-start(bf16[1,128,2048]{2,1,0:T(8,128)(2,1)} %param.6) | copy-start | bytes 1572868
  27.7 15.5 %all-to-all-start = ((bf16[8,1,192]{2,1,0:T(2,128)(2,1)}), bf16[8,1,192]{2,1,0:T(2,128)(2,1)S(1)}, u32[]{:S(2)}, u32[]{:S(2)}) async-start(bf16[8,1,192]{2,1,0:T(2,128)(2,1)} %all_to_all.20), calls=%async_computation | async-start | bytes 16384 | tf_op jit(solution)/shard_map/all_to_all | solution.py:43
  43.1 76.5 %copy-start.4 = (bf16[1,4,8,48,768]{4,3,2,1,0:T(8,128)(2,1)S(1)}, bf16[1,4,8,48,768]{4,3,2,1,0:T(8,128)(2,1)}, u32[]{:S(2)}) copy-start(bf16[1,4,8,48,768]{4,3,2,1,0:T(8,128)(2,1)} %param.10) | copy-start | bytes 7077892
  43.1 76.5 %all-to-all-start.1 = ((bf16[8,192,2048]{2,1,0:T(8,128)(2,1)}), bf16[8,192,2048]{2,1,0:T(8,128)(2,1)}, u32[]{:S(2)}, u32[]{:S(2)}) async-start(bf16[8,192,2048]{2,1,0:T(8,128)(2,1)} %bitcast.46), calls=%async_computation.1 | async-start | bytes 12582912 | tf_op jit(solution)/shard_map/all_to_all | solution.py:36
  48.1 556.8 %reduce-scatter.2.cloned.1.call-start = ((), (), s32[]{:S(2)}) async-start(), calls=%async_computation.4 | async-start | bytes 15728640 | tf_op jit(solution)/shard_map/reduce_scatter | solution.py:64
  152.0 194.9 %collective-permute-start = (bf16[512,3072]{0,1:T(8,128)(2,1)S(1)}, bf16[512,3072]{0,1:T(8,128)(2,1)S(1)}, u32[]{:S(2)}, u32[]{:S(2)}) collective-permute-start(bf16[512,3072]{0,1:T(8,128)(2,1)S(1)} %copy.32), channel_id=1, source_target_pairs={{0,3},{1,0},{2,1},{3,2},{4,7},{5,4},{6,5},{7,6},{8,11},{9,8},{10,9... | collective-permute-start | bytes 9437192 | tf_op jit(solution)/shard_map/ppermute | solution.py:12
  346.9 1.7 copy-start.2
  348.6 142.0 %collective-permute-start.1 = (bf16[512,3072]{0,1:T(8,128)(2,1)S(1)}, bf16[512,3072]{0,1:T(8,128)(2,1)}, u32[]{:S(2)}, u32[]{:S(2)}) collective-permute-start(bf16[512,3072]{0,1:T(8,128)(2,1)S(1)} %collective-permute-done), channel_id=1, source_target_pairs={{0,3},{1,0},{2,1},{3,2},{4,7},{5,4},{6,5},{7,6},{8,11},{9,8},{10,9... | collective-permute-start | bytes 9437192 | tf_op jit(solution)/shard_map/ppermute | solution.py:12
  490.5 67.0 %collective-permute-start.2 = (bf16[512,3072]{0,1:T(8,128)(2,1)}, bf16[512,3072]{0,1:T(8,128)(2,1)}, u32[]{:S(2)}, u32[]{:S(2)}) collective-permute-start(bf16[512,3072]{0,1:T(8,128)(2,1)} %collective-permute-done.1), channel_id=1, source_target_pairs={{0,3},{1,0},{2,1},{3,2},{4,7},{5,4},{6,5},{7,6},{8,11},{9,8},{10,9... | collective-permute-start | bytes 9437192 | tf_op jit(solution)/shard_map/ppermute | solution.py:12
  490.5 1.9 copy-start.3
  565.7 5.5 copy-start.5
  587.2 10.6 %all-to-all-start.2 = ((f32[8,1,192]{2,1,0:T(1,128)}), f32[8,1,192]{2,1,0:T(1,128)S(1)}, u32[]{:S(2)}, u32[]{:S(2)}) async-start(f32[8,1,192]{2,1,0:T(1,128)} %all_to_all.21), calls=%async_computation.2 | async-start | bytes 16384 | tf_op jit(solution)/shard_map/all_to_all | solution.py:54
  597.9 12.4 %copy-start.1 = (bf16[1,128,2048]{2,1,0:T(8,128)(2,1)S(1)}, bf16[1,128,2048]{2,1,0:T(8,128)(2,1)}, u32[]{:S(2)}) copy-start(bf16[1,128,2048]{2,1,0:T(8,128)(2,1)} %param.6) | copy-start | bytes 1572868
Sparse Core Ops, SparseCore 0:
  148.9 348.1 reduce-scatter.1
